TPU v7x, 32 devices: a whole 2x2x4 slice. The times are simulated.
32 devices in a mesh: ctx: 8 (over z, x), wt: 4 (over y, core).
Axes of the slice: x: 2, y: 2, z: 4, core: 2. Of those that a mesh axis runs over, the one named last changes fastest.
Arguments:
- hidden_in: bfloat16 [2, 4, 1024, 960], P(None, 'wt', 'ctx'), may hold values from -6 to 6
- d_out: bfloat16 [2, 4, 1024, 960], P(None, 'wt', 'ctx'), may hold values from -6 to 6
- block_order: int32 [2, 16], replicated, may hold values from 0 to 15, as said below
- gain_attn: bfloat16 [960], P('wt'), may hold values from 0.5 to 1.5
- gain_mlp: bfloat16 [960], P('wt'), may hold values from 0.5 to 1.5
- w_q: bfloat16 [960, 960], P('wt'), may hold values from -0.25 to 0.25
- w_kv: bfloat16 [960, 640], P('wt'), may hold values from -0.1875 to 0.1875
- w_o: bfloat16 [960, 960], P('wt'), may hold values from -3 to 3
- w_gu: bfloat16 [960, 5120], P('wt'), may hold values from -0.1875 to 0.1875
- w_down: bfloat16 [2560, 960], P('wt'), may hold values from -0.25 to 0.25
Outputs:
- hidden_out: bfloat16 [2, 4, 1024, 960], P(None, 'wt', 'ctx')
- grad_in: bfloat16 [2, 4, 1024, 960], P(None, 'wt', 'ctx')
- grad_gain_attn: float32 [960], P('wt')
- grad_gain_mlp: float32 [960], P('wt')
- grad_w_q: float32 [960, 960], P('wt')
- grad_w_kv: float32 [960, 640], P('wt')
- grad_w_o: float32 [960, 960], P('wt')
- grad_w_gu: float32 [960, 5120], P('wt')
- grad_w_down: float32 [2560, 960], P('wt')
Inputs may be any that keep to these rules, and one draw needn't show every extreme that they name: block_order[m] is a permutation of the 16 blocks in which stored blocks 2c and 2c + 1 are a mirrored pair: their numbers add up to 15.
All inputs are finite; a program needn't handle non-finite values.
Results may differ from a plain program's by a relative error of at most 0.018.
Values may be sent and summed in bfloat16 or wider, within the bound.
A program may use at most 256 MiB of HBM per device.

v0:
```python
import math

import jax
import jax.numpy as jnp
from jax import lax
from jax.sharding import PartitionSpec as P

QH = 15
KVH = 5
HD = 64


eps_norm = 1e-05
rope_base = 10000.0


def norm_scale(values, gain):
    return values * lax.rsqrt(jnp.mean(values * values, axis=-1, keepdims=True) + eps_norm) * gain


def rope_tables(positions):
    half_dim = HD // 2
    frequency = jnp.exp(jnp.arange(half_dim, dtype=jnp.float32) * (-2.0 * math.log(rope_base) / HD))
    angles = positions.astype(jnp.float32)[:, None] * frequency[None, :]
    return (jnp.cos(angles), jnp.sin(angles))


def rotate(values, cosine, sine):
    half_dim = values.shape[-1] // 2
    first_half = values[..., :half_dim]
    second_half = values[..., half_dim:]
    cos_wide = cosine[:, None, :]
    sin_wide = sine[:, None, :]
    return jnp.concatenate(
        [
            first_half * cos_wide - second_half * sin_wide,
            second_half * cos_wide + first_half * sin_wide,
        ],
        axis=-1,
    )


def unrotate(values, cosine, sine):
    half_dim = values.shape[-1] // 2
    first_half = values[..., :half_dim]
    second_half = values[..., half_dim:]
    cos_wide = cosine[:, None, :]
    sin_wide = sine[:, None, :]
    return jnp.concatenate(
        [
            first_half * cos_wide + second_half * sin_wide,
            second_half * cos_wide - first_half * sin_wide,
        ],
        axis=-1,
    )


def block_size(total_rows, limit):
    best_size = 1
    for candidate in range(1, min(total_rows, limit) + 1):
        if total_rows % candidate == 0:
            best_size = candidate
    return best_size


def outer_sum(left, right):
    return lax.dot_general(
        left, right, (((0,), (0,)), ((), ())), preferred_element_type=jnp.float32
    )


def back_product(left, weight):
    return lax.dot_general(
        left, weight, (((1,), (1,)), ((), ())), preferred_element_type=jnp.float32
    )


def block_scores(query_groups, keys_block, key_pos, row_pos, score_scale):
    scores = (
        jnp.einsum("hrd,khd->hrk", query_groups, keys_block, preferred_element_type=jnp.float32)
        * score_scale
    )
    visible = key_pos[None, None, :] <= row_pos[None, :, None]
    return (scores, visible)


def local(hidden_in, d_out, block_order, gain_attn, gain_mlp, w_q, w_kv, w_o, w_gu, w_down):
    gathered = (
        lax.all_gather(gain_attn, "wt", axis=0, tiled=True),
        lax.all_gather(gain_mlp, "wt", axis=0, tiled=True),
        lax.all_gather(w_q, "wt", axis=0, tiled=True),
        lax.all_gather(w_kv, "wt", axis=0, tiled=True),
        lax.all_gather(w_o, "wt", axis=0, tiled=True),
        lax.all_gather(w_gu, "wt", axis=0, tiled=True),
        lax.all_gather(w_down, "wt", axis=0, tiled=True),
    )
    gain_one = gathered[0].astype(jnp.float32)
    gain_two = gathered[1].astype(jnp.float32)
    weight_q, weight_kv, weight_o, weight_gu, weight_down = (
        gathered[2],
        gathered[3],
        gathered[4],
        gathered[5],
        gathered[6],
    )
    micro_count = hidden_in.shape[0]
    seg_rows = hidden_in.shape[2]
    n_ctx = lax.axis_size("ctx")
    seq_len = seg_rows * n_ctx
    half_block = seg_rows // 2
    kv_width = KVH * HD
    group_size = QH // KVH
    row_count = group_size * seg_rows
    ff_width = weight_down.shape[0]
    key_block = block_size(seq_len, 1024)
    block_count = seq_len // key_block
    score_scale = 1.0 / math.sqrt(HD)
    my_start = lax.axis_index("ctx") * seg_rows
    grad_names = [jnp.zeros(item.shape, jnp.float32) for item in gathered]
    outputs = []
    input_grads = []
    for micro_index in range(micro_count):
        tokens_in = hidden_in[micro_index, 0].astype(jnp.float32)
        order_row = block_order[micro_index]
        key_pos = (
            order_row[:, None] * half_block + jnp.arange(half_block, dtype=jnp.int32)[None, :]
        ).reshape(seq_len)
        query_pos = lax.dynamic_slice_in_dim(key_pos, my_start, seg_rows)
        row_pos = jnp.tile(query_pos, group_size)
        cosine, sine = rope_tables(query_pos)
        normed_one, pull_one = jax.vjp(norm_scale, tokens_in, gain_one)
        act_one = normed_one.astype(jnp.bfloat16)
        query_lin = jnp.dot(act_one, weight_q, preferred_element_type=jnp.float32).reshape(
            seg_rows, QH, HD
        )
        query_rot = rotate(query_lin, cosine, sine).astype(jnp.bfloat16)
        query_groups = (
            query_rot.reshape(seg_rows, KVH, group_size, HD)
            .transpose(1, 2, 0, 3)
            .reshape(KVH, row_count, HD)
        )
        kv_lin = jnp.dot(act_one, weight_kv, preferred_element_type=jnp.float32)
        key_rot = rotate(kv_lin[:, :kv_width].reshape(seg_rows, KVH, HD), cosine, sine).reshape(
            seg_rows, kv_width
        )
        kv_send = jnp.concatenate([key_rot, kv_lin[:, kv_width:]], axis=1).astype(jnp.bfloat16)
        kv_whole = lax.all_gather(kv_send, "ctx", axis=0, tiled=True)
        kv_blocks = kv_whole.reshape(block_count, key_block, 2 * kv_width)
        pos_blocks = key_pos.reshape(block_count, key_block)

        def lse_step(carry, item):
            top_now, total_now = carry
            kv_block, kpos = item
            keys_block = kv_block[:, :kv_width].reshape(key_block, KVH, HD)
            scores, visible = block_scores(query_groups, keys_block, kpos, row_pos, score_scale)
            top_new = jnp.maximum(top_now, jnp.max(jnp.where(visible, scores, -1e30), axis=-1))
            total_new = total_now * jnp.exp(top_now - top_new) + jnp.sum(
                jnp.where(visible, jnp.exp(scores - top_new[..., None]), 0.0), axis=-1
            )
            return ((top_new, total_new), None)

        start_top = jnp.full((KVH, row_count), -1e30, jnp.float32)
        start_total = jnp.zeros((KVH, row_count), jnp.float32)
        (top_all, total_all), _ = lax.scan(
            lse_step, (start_top, start_total), (kv_blocks, pos_blocks)
        )
        lse = top_all + jnp.log(total_all)

        def value_step(acc_now, item):
            kv_block, kpos = item
            keys_block = kv_block[:, :kv_width].reshape(key_block, KVH, HD)
            vals_block = kv_block[:, kv_width:].reshape(key_block, KVH, HD)
            scores, visible = block_scores(query_groups, keys_block, kpos, row_pos, score_scale)
            probs = jnp.where(visible, jnp.exp(scores - lse[..., None]), 0.0).astype(jnp.bfloat16)
            return (
                acc_now
                + jnp.einsum("hrk,khd->hrd", probs, vals_block, preferred_element_type=jnp.float32),
                None,
            )

        acc_all, _ = lax.scan(
            value_step, jnp.zeros((KVH, row_count, HD), jnp.float32), (kv_blocks, pos_blocks)
        )
        attn_low = (
            acc_all.reshape(KVH, group_size, seg_rows, HD)
            .transpose(2, 0, 1, 3)
            .reshape(seg_rows, QH * HD)
            .astype(jnp.bfloat16)
        )
        mid_state = tokens_in + jnp.dot(attn_low, weight_o, preferred_element_type=jnp.float32)
        normed_two, pull_two = jax.vjp(norm_scale, mid_state, gain_two)
        act_two = normed_two.astype(jnp.bfloat16)
        gate_up = jnp.dot(act_two, weight_gu, preferred_element_type=jnp.float32)
        gate_part = gate_up[:, :ff_width]
        up_part = gate_up[:, ff_width:]
        sig_gate = jax.nn.sigmoid(gate_part)
        hidden_low = (gate_part * sig_gate * up_part).astype(jnp.bfloat16)
        result = mid_state + jnp.dot(hidden_low, weight_down, preferred_element_type=jnp.float32)
        outputs.append(result.astype(jnp.bfloat16))
        grad_low = d_out[micro_index, 0]
        grad_top = grad_low.astype(jnp.float32)
        grad_down = outer_sum(hidden_low, grad_low)
        d_hidden = back_product(grad_low, weight_down)
        d_gate = d_hidden * up_part * sig_gate * (1.0 + gate_part * (1.0 - sig_gate))
        d_up = d_hidden * gate_part * sig_gate
        d_gu_low = jnp.concatenate([d_gate, d_up], axis=1).astype(jnp.bfloat16)
        grad_gu = outer_sum(act_two, d_gu_low)
        d_act_two = back_product(d_gu_low, weight_gu)
        d_mid_norm, grad_gain_two = pull_two(d_act_two)
        d_mid = grad_top + d_mid_norm
        d_mid_low = d_mid.astype(jnp.bfloat16)
        grad_o = outer_sum(attn_low, d_mid_low)
        d_attn_low = back_product(d_mid_low, weight_o).astype(jnp.bfloat16)
        grad_groups = (
            d_attn_low.reshape(seg_rows, KVH, group_size, HD)
            .transpose(1, 2, 0, 3)
            .reshape(KVH, row_count, HD)
        )
        kv_back = lax.all_gather(kv_send, "ctx", axis=0, tiled=True).reshape(
            block_count, key_block, 2 * kv_width
        )

        def delta_step(delta_now, item):
            kv_block, kpos = item
            keys_block = kv_block[:, :kv_width].reshape(key_block, KVH, HD)
            vals_block = kv_block[:, kv_width:].reshape(key_block, KVH, HD)
            scores, visible = block_scores(query_groups, keys_block, kpos, row_pos, score_scale)
            probs = jnp.where(visible, jnp.exp(scores - lse[..., None]), 0.0)
            d_probs = jnp.einsum(
                "hrd,khd->hrk", grad_groups, vals_block, preferred_element_type=jnp.float32
            )
            return (delta_now + jnp.sum(probs * d_probs, axis=-1), None)

        delta, _ = lax.scan(
            delta_step, jnp.zeros((KVH, row_count), jnp.float32), (kv_back, pos_blocks)
        )

        def grad_step(dq_now, item):
            kv_block, kpos = item
            keys_block = kv_block[:, :kv_width].reshape(key_block, KVH, HD)
            vals_block = kv_block[:, kv_width:].reshape(key_block, KVH, HD)
            scores, visible = block_scores(query_groups, keys_block, kpos, row_pos, score_scale)
            probs = jnp.where(visible, jnp.exp(scores - lse[..., None]), 0.0)
            d_probs = jnp.einsum(
                "hrd,khd->hrk", grad_groups, vals_block, preferred_element_type=jnp.float32
            )
            d_scores = (probs * (d_probs - delta[..., None])).astype(jnp.bfloat16)
            dq_new = dq_now + jnp.einsum(
                "hrk,khd->hrd", d_scores, keys_block, preferred_element_type=jnp.float32
            )
            d_keys = (
                jnp.einsum(
                    "hrk,hrd->khd", d_scores, query_groups, preferred_element_type=jnp.float32
                )
                * score_scale
            )
            d_vals = jnp.einsum(
                "hrk,hrd->khd",
                probs.astype(jnp.bfloat16),
                grad_groups,
                preferred_element_type=jnp.float32,
            )
            return (
                dq_new,
                jnp.concatenate(
                    [d_keys.reshape(key_block, kv_width), d_vals.reshape(key_block, kv_width)],
                    axis=1,
                ),
            )

        dq_groups, dkv_blocks = lax.scan(
            grad_step, jnp.zeros((KVH, row_count, HD), jnp.float32), (kv_back, pos_blocks)
        )
        dkv_mine = lax.psum_scatter(
            dkv_blocks.reshape(seq_len, 2 * kv_width), "ctx", scatter_dimension=0, tiled=True
        )
        d_query = (
            (dq_groups * score_scale)
            .reshape(KVH, group_size, seg_rows, HD)
            .transpose(2, 0, 1, 3)
            .reshape(seg_rows, QH, HD)
        )
        d_q_low = unrotate(d_query, cosine, sine).reshape(seg_rows, QH * HD).astype(jnp.bfloat16)
        d_key = unrotate(dkv_mine[:, :kv_width].reshape(seg_rows, KVH, HD), cosine, sine).reshape(
            seg_rows, kv_width
        )
        d_kv_low = jnp.concatenate([d_key, dkv_mine[:, kv_width:]], axis=1).astype(jnp.bfloat16)
        grad_q = outer_sum(act_one, d_q_low)
        grad_kv = outer_sum(act_one, d_kv_low)
        d_act_one = back_product(d_q_low, weight_q) + back_product(d_kv_low, weight_kv)
        d_in_norm, grad_gain_one = pull_one(d_act_one)
        input_grads.append((d_mid + d_in_norm).astype(jnp.bfloat16))
        parts_now = [grad_gain_one, grad_gain_two, grad_q, grad_kv, grad_o, grad_gu, grad_down]
        grad_names = [total + piece for total, piece in zip(grad_names, parts_now)]
    owned = (
        lax.psum_scatter(
            grad_names[0].astype(jnp.bfloat16), "wt", scatter_dimension=0, tiled=True
        ).astype(jnp.float32),
        lax.psum_scatter(
            grad_names[1].astype(jnp.bfloat16), "wt", scatter_dimension=0, tiled=True
        ).astype(jnp.float32),
        lax.psum_scatter(
            grad_names[2].astype(jnp.bfloat16), "wt", scatter_dimension=0, tiled=True
        ).astype(jnp.float32),
        lax.psum_scatter(
            grad_names[3].astype(jnp.bfloat16), "wt", scatter_dimension=0, tiled=True
        ).astype(jnp.float32),
        lax.psum_scatter(
            grad_names[4].astype(jnp.bfloat16), "wt", scatter_dimension=0, tiled=True
        ).astype(jnp.float32),
        lax.psum_scatter(
            grad_names[5].astype(jnp.bfloat16), "wt", scatter_dimension=0, tiled=True
        ).astype(jnp.float32),
        lax.psum_scatter(
            grad_names[6].astype(jnp.bfloat16), "wt", scatter_dimension=0, tiled=True
        ).astype(jnp.float32),
    )
    summed = lax.psum((owned[0], owned[1], owned[2], owned[3], owned[4], owned[5], owned[6]), "ctx")
    hidden_out = jnp.stack(outputs)[:, None]
    grad_in = jnp.stack(input_grads)[:, None]
    return (
        hidden_out,
        grad_in,
        summed[0],
        summed[1],
        summed[2],
        summed[3],
        summed[4],
        summed[5],
        summed[6],
    )


def solution(mesh):
    placed = (
        P(None, "wt", "ctx", None),
        P(None, "wt", "ctx", None),
        P(),
        P("wt"),
        P("wt"),
        P("wt", None),
        P("wt", None),
        P("wt", None),
        P("wt", None),
        P("wt", None),
    )
    return jax.shard_map(
        local,
        mesh=mesh,
        in_specs=placed,
        out_specs=(
            P(None, "wt", "ctx", None),
            P(None, "wt", "ctx", None),
            P("wt"),
            P("wt"),
            P("wt", None),
            P("wt", None),
            P("wt", None),
            P("wt", None),
            P("wt", None),
        ),
        check_vma=False,
    )
```

profile of v0, /device:TPU:0, one launch (start us, length us, event | category | flops | bytes accessed | tf_op | source)
XLA Modules:
  0.0 1084.1 jit_solution(5646645169143521290)
XLA Ops:
  12.4 8.3 all-reduce.6
  23.4 6.6 all-gather.10.cloned.1.call-done
  37.8 15.7 %all-gather.8.cloned.1.call-done = bf16[960,960]{1,0:T(8,128)(2,1)} async-done(((bf16[240,960]{1,0:T(8,128)(2,1)}), bf16[960,960]{1,0:T(8,128)(2,1)}) %all-gather.8.cloned.1.call-update) | async-done | bytes 1843216 | tf_op jit(solution)/shard_map/all_gather | solution.py:91
  59.6 38.7 %all-gather.20.cloned.1.call-done = bf16[1024,640]{1,0:T(8,128)(2,1)} async-done(((bf16[128,640]{1,0:T(8,128)(2,1)}), bf16[1024,640]{1,0:T(8,128)(2,1)}) %all-gather.20.cloned.1.call-update) | async-done | bytes 1310736 | tf_op jit(solution)/shard_map/all_gather | solution.py:147
  110.2 31.5 %all-gather.12.cloned.1.call-done = bf16[1024,640]{1,0:T(8,128)(2,1)} async-done(((bf16[128,640]{1,0:T(8,128)(2,1)}), bf16[1024,640]{1,0:T(8,128)(2,1)}) %all-gather.12.cloned.1.call-update) | async-done | bytes 1310736 | tf_op jit(solution)/shard_map/all_gather | solution.py:147
  152.6 11.0 %all-gather.14.cloned.1.call-done = bf16[960,960]{1,0:T(8,128)(2,1)} async-done(((bf16[240,960]{1,0:T(8,128)(2,1)}), bf16[960,960]{1,0:T(8,128)(2,1)}) %all-gather.14.cloned.1.call-update) | async-done | bytes 1843216 | tf_op jit(solution)/shard_map/all_gather | solution.py:93
  168.5 63.0 %all-gather.16.cloned.1.call-done = bf16[960,5120]{1,0:T(8,128)(2,1)} async-done(((bf16[240,5120]{1,0:T(8,128)(2,1)}), bf16[960,5120]{1,0:T(8,128)(2,1)}) %all-gather.16.cloned.1.call-update) | async-done | bytes 9830416 | tf_op jit(solution)/shard_map/all_gather | solution.py:94
  231.6 7.1 fusion.88
  241.8 29.9 %all-gather.18.cloned.1.call-done = bf16[2560,960]{0,1:T(8,128)(2,1)} async-done(((bf16[640,960]{0,1:T(8,128)(2,1)}), bf16[2560,960]{0,1:T(8,128)(2,1)}) %all-gather.18.cloned.1.call-update) | async-done | bytes 4915216 | tf_op jit(solution)/shard_map/all_gather | solution.py:95
  271.7 5.5 multiply_convert_fusion.3
  277.2 5.2 multiply_convert_fusion.5
  294.3 6.6 multiply_reduce_fusion
  300.9 5.1 fusion.89
  306.0 4.5 multiply_convert_fusion
  317.3 6.8 multiply_reduce_fusion.1
  324.1 4.6 multiply_convert_fusion.1
  333.5 3.5 convolution_multiply_fusion.2
  337.3 4.3 convolution_multiply_fusion.3
  349.1 37.0 %reduce-scatter.12.cloned.1.call-done = f32[128,640]{0,1:T(8,128)} async-done(((f32[1024,640]{0,1:T(8,128)}), f32[128,640]{0,1:T(8,128)}) %reduce-scatter.12.cloned.1.call-update) | async-done | bytes 327696 | tf_op jit(solution)/shard_map/reduce_scatter | solution.py:274
  388.0 71.2 %reduce-scatter.10.cloned.1.call-done = f32[128,640]{0,1:T(8,128)} async-done(((f32[1024,640]{0,1:T(8,128)}), f32[128,640]{0,1:T(8,128)}) %reduce-scatter.10.cloned.1.call-update) | async-done | bytes 327696 | tf_op jit(solution)/shard_map/reduce_scatter | solution.py:274
  466.4 3.7 add_convert_fusion.1
  470.1 7.9 copy.86
  478.0 9.6 fusion.7
  487.6 11.8 %add_convert_fusion = bf16[960,5120]{1,0:T(8,128)(2,1)} fusion(f32[960,5120]{1,0:T(8,128)} %fusion.7, bf16[128,2560]{1,0:T(8,128)(2,1)} %copy-done.46, bf16[128,2560]{1,0:T(8,128)(2,1)} %copy-done.45, f32[128,960]{0,1:T(8,128)S(1)} %get-tuple-element.300, f32[128]{0:T(128)S(1)} %fusion.78, f32[960]{0:T(1024)S(1)} %convert_element_type.227), kind=kOutput, calls=%fused_computation | convolution fusion | flops 1271111680 | bytes 31297792 | tf_op jit(solution)/shard_map/dot_general | solution.py:67
  500.1 4.1 fusion.4
  504.3 4.2 fusion.5
  512.3 12.9 %reduce-scatter.18.cloned.1.call-done = bf16[240,960]{1,0:T(8,128)(2,1)} async-done(((bf16[960,960]{1,0:T(8,128)(2,1)}), bf16[240,960]{1,0:T(8,128)(2,1)}) %reduce-scatter.18.cloned.1.call-update) | async-done | bytes 460816 | tf_op jit(solution)/shard_map/reduce_scatter | solution.py:308
  529.2 5.7 all-reduce.5
  537.3 16.5 %reduce-scatter.16.cloned.1.call-done = bf16[240,640]{1,0:T(8,128)(2,1)} async-done(((bf16[960,640]{1,0:T(8,128)(2,1)}), bf16[240,640]{1,0:T(8,128)(2,1)}) %reduce-scatter.16.cloned.1.call-update) | async-done | bytes 307216 | tf_op jit(solution)/shard_map/reduce_scatter | solution.py:305
  553.8 54.1 %reduce-scatter.22.cloned.1.call-done = bf16[640,960]{1,0:T(8,128)(2,1)} async-done(((bf16[2560,960]{1,0:T(8,128)(2,1)}), bf16[640,960]{1,0:T(8,128)(2,1)}) %reduce-scatter.22.cloned.1.call-update) | async-done | bytes 1228816
  610.0 81.4 %reduce-scatter.20.cloned.1.call-done = bf16[240,5120]{1,0:T(8,128)(2,1)} async-done(((bf16[960,5120]{1,0:T(8,128)(2,1)}), bf16[240,5120]{1,0:T(8,128)(2,1)}) %reduce-scatter.20.cloned.1.call-update) | async-done | bytes 2457616 | tf_op jit(solution)/shard_map/reduce_scatter | solution.py:311
  691.4 385.8 %all-reduce.8 = (f32[240]{0:T(256)}, f32[240]{0:T(256)}, f32[240,960]{1,0:T(8,128)}, f32[240,640]{1,0:T(8,128)}, f32[240,960]{1,0:T(8,128)}, /*index=5*/f32[240,5120]{1,0:T(8,128)}, f32[640,960]{0,1:T(8,128)}) all-reduce(f32[240]{0:T(256)S(1)} %get-tuple-element.314, ...), channel_id=1, replica_groups=mesh['ctx'=8,'wt'=4] {'ctx'}, use_global_device_ids=true, to_apply=%region_19.20 | all-reduce | flops 2458080 | bytes 14749440 | tf_op jit(solution)/shard_map/psum | solution.py:318
  (299 shorter events, 103.1 us)
Async XLA Ops:
  7.2 26.2 %copy-start.6 = (bf16[2,1,128,960]{2,3,1,0:T(8,128)(2,1)S(1)}, bf16[2,1,128,960]{2,3,1,0:T(8,128)(2,1)}, u32[]{:S(2)}) copy-start(bf16[2,1,128,960]{2,3,1,0:T(8,128)(2,1)} %param.10) | copy-start | bytes 1474564
  7.2 22.9 %all-gather.10.cloned.1.call-start = ((), (), s32[]{:S(2)}) async-start(), calls=%async_computation.8 | async-start | bytes 1536000 | tf_op jit(solution)/shard_map/all_gather | solution.py:92
  7.9 45.6 %all-gather.8.cloned.1.call-start = ((), (), s32[]{:S(2)}) async-start(), calls=%async_computation.7 | async-start | bytes 2457600 | tf_op jit(solution)/shard_map/all_gather | solution.py:91
  8.7 89.7 %all-gather.20.cloned.1.call-start = ((), (), s32[]{:S(2)}) async-start(), calls=%async_computation.13 | async-start | bytes 1474560 | tf_op jit(solution)/shard_map/all_gather | solution.py:147
  23.2 12.0 %copy-start.63 = (f32[128]{0:T(128)}, f32[128]{0:T(128)S(1)}, u32[]{:S(2)}) copy-start(f32[128]{0:T(128)S(1)} %get-tuple-element.219) | copy-start | bytes 1540
  23.4 34.7 %copy-start.49 = (f32[128,32]{0,1:T(8,128)}, f32[128,32]{0,1:T(8,128)S(1)}, u32[]{:S(2)}) copy-start(f32[128,32]{0,1:T(8,128)S(1)} %get-tuple-element.295) | copy-start | bytes 49156
  23.4 34.7 %copy-start.51 = (f32[128,32]{0,1:T(8,128)}, f32[128,32]{0,1:T(8,128)S(1)}, u32[]{:S(2)}) copy-start(f32[128,32]{0,1:T(8,128)S(1)} %get-tuple-element.296) | copy-start | bytes 49156
  33.3 108.4 %all-gather.12.cloned.1.call-start = ((), (), s32[]{:S(2)}) async-start(), calls=%async_computation.9 | async-start | bytes 1474560 | tf_op jit(solution)/shard_map/all_gather | solution.py:147
  35.2 128.5 %all-gather.14.cloned.1.call-start = ((), (), s32[]{:S(2)}) async-start(), calls=%async_computation.10 | async-start | bytes 2457600 | tf_op jit(solution)/shard_map/all_gather | solution.py:93
  35.8 195.8 %all-gather.16.cloned.1.call-start = ((), (), s32[]{:S(2)}) async-start(), calls=%async_computation.11 | async-start | bytes 12288000 | tf_op jit(solution)/shard_map/all_gather | solution.py:94
  36.4 235.3 %all-gather.18.cloned.1.call-start = ((), (), s32[]{:S(2)}) async-start(), calls=%async_computation.12 | async-start | bytes 6144000 | tf_op jit(solution)/shard_map/all_gather | solution.py:95
  37.1 349.0 %reduce-scatter.12.cloned.1.call-start = ((), (), s32[]{:S(2)}) async-start(), calls=%async_computation.15 | async-start | bytes 2949120 | tf_op jit(solution)/shard_map/reduce_scatter | solution.py:274
  37.5 70.0 %copy-start.12 = (pred[384,1024]{1,0:T(8,128)(4,1)}, pred[384,1024]{1,0:T(8,128)(4,1)S(1)}, u32[]{:S(2)}) copy-start(pred[384,1024]{1,0:T(8,128)(4,1)S(1)} %broadcast_compare_fusion) | copy-start | bytes 1179652
  37.8 112.5 %copy-start.10 = (pred[384,1024]{1,0:T(8,128)(4,1)}, pred[384,1024]{1,0:T(8,128)(4,1)S(1)}, u32[]{:S(2)}) copy-start(pred[384,1024]{1,0:T(8,128)(4,1)S(1)} %broadcast_compare_fusion.1) | copy-start | bytes 1179652
  59.0 46.1 %copy-start.37 = (bf16[5,384,64]{1,2,0:T(8,128)(2,1)}, bf16[5,384,64]{1,2,0:T(8,128)(2,1)S(1)}, u32[]{:S(2)}) copy-start(bf16[5,384,64]{1,2,0:T(8,128)(2,1)S(1)} %reshape.569) | copy-start | bytes 737284
  59.6 86.4 %copy-start.35 = (bf16[5,384,64]{1,2,0:T(8,128)(2,1)}, bf16[5,384,64]{1,2,0:T(8,128)(2,1)S(1)}, u32[]{:S(2)}) copy-start(bf16[5,384,64]{1,2,0:T(8,128)(2,1)S(1)} %reshape.564) | copy-start | bytes 737284
  110.2 53.5 %copy-start.29 = (bf16[128,5,3,64]{0,3,2,1:T(8,128)(2,1)}, bf16[128,5,3,64]{0,3,2,1:T(8,128)(2,1)S(1)}, u32[]{:S(2)}) copy-start(bf16[128,5,3,64]{0,3,2,1:T(8,128)(2,1)S(1)} %copy.79) | copy-start | bytes 737284
  152.6 86.0 %copy-start.31 = (bf16[128,5,3,64]{0,3,2,1:T(8,128)(2,1)}, bf16[128,5,3,64]{0,3,2,1:T(8,128)(2,1)S(1)}, u32[]{:S(2)}) copy-start(bf16[128,5,3,64]{0,3,2,1:T(8,128)(2,1)S(1)} %copy.72) | copy-start | bytes 737284
  238.7 33.0 %copy-start.26 = (bf16[2,1,128,960]{2,3,1,0:T(8,128)(2,1)S(1)}, bf16[2,1,128,960]{2,3,1,0:T(8,128)(2,1)}, u32[]{:S(2)}) copy-start(bf16[2,1,128,960]{2,3,1,0:T(8,128)(2,1)} %param.11) | copy-start | bytes 1474564
  315.0 144.2 %reduce-scatter.10.cloned.1.call-start = ((), (), s32[]{:S(2)}) async-start(), calls=%async_computation.14 | async-start | bytes 2949120 | tf_op jit(solution)/shard_map/reduce_scatter | solution.py:274
  317.2 12.3 %slice-start = ((s8[7864320]{0:T(1024)(128)(4,1)}), s8[4194304]{0:T(1024)(128)(4,1)S(1)}, s32[]{:S(2)}) async-start(s8[7864320]{0:T(1024)(128)(4,1)} %bitcast.245), calls=%async_computation.21 | async-start | bytes 8388608
  333.4 178.9 %reduce-scatter.14.cloned.1.call-start = ((), (), s32[]{:S(2)}) async-start(), calls=%async_computation.16 | async-start | bytes 2457600 | tf_op jit(solution)/shard_map/reduce_scatter | solution.py:302
  346.0 179.3 %reduce-scatter.18.cloned.1.call-start = ((), (), s32[]{:S(2)}) async-start(), calls=%async_computation.18 | async-start | bytes 2457600 | tf_op jit(solution)/shard_map/reduce_scatter | solution.py:308
  349.1 204.7 %reduce-scatter.16.cloned.1.call-start = ((), (), s32[]{:S(2)}) async-start(), calls=%async_computation.17 | async-start | bytes 1536000 | tf_op jit(solution)/shard_map/reduce_scatter | solution.py:305
  387.1 76.4 %copy-start.42 = (bf16[128,320]{0,1:T(8,128)(2,1)}, bf16[128,320]{0,1:T(8,128)(2,1)S(1)}, u32[]{:S(2)}) copy-start(bf16[128,320]{0,1:T(8,128)(2,1)S(1)} %slice.310) | copy-start | bytes 245764
  463.5 144.4 %reduce-scatter.22.cloned.1.call-start = ((), (), s32[]{:S(2)}) async-start(), calls=%async_computation.20 | async-start | bytes 6553600
  478.0 213.4 %reduce-scatter.20.cloned.1.call-start = ((), (), s32[]{:S(2)}) async-start(), calls=%async_computation.19 | async-start | bytes 12288000 | tf_op jit(solution)/shard_map/reduce_scatter | solution.py:311
  508.5 16.8 %copy-start.9 = (bf16[960,640]{1,0:T(8,128)(2,1)S(1)}, bf16[960,640]{1,0:T(8,128)(2,1)}, u32[]{:S(2)}) copy-start(bf16[960,640]{1,0:T(8,128)(2,1)} %all-gather.10.cloned.1.call-done) | copy-start | bytes 3686404
  508.5 16.8 %copy-start.43 = (bf16[128,320]{0,1:T(8,128)(2,1)S(1)}, bf16[128,320]{0,1:T(8,128)(2,1)}, u32[]{:S(2)}) copy-start(bf16[128,320]{0,1:T(8,128)(2,1)} %copy-done.42) | copy-start | bytes 245764
  510.8 24.3 %copy-start.62 = (f32[128]{0:T(128)S(1)}, f32[128]{0:T(128)}, u32[]{:S(2)}) copy-start(f32[128]{0:T(128)} %copy-done.61) | copy-start | bytes 1540
  510.8 24.3 %copy-start.64 = (f32[128]{0:T(128)S(1)}, f32[128]{0:T(128)}, u32[]{:S(2)}) copy-start(f32[128]{0:T(128)} %copy-done.63) | copy-start | bytes 1540
  510.8 24.3 %copy-start.17 = (f32[128,960]{0,1:T(8,128)S(1)}, f32[128,960]{0,1:T(8,128)}, u32[]{:S(2)}) copy-start(f32[128,960]{0,1:T(8,128)} %copy-done.15) | copy-start | bytes 1474564
  (52 other events, 216.6 us)
Sparse Core Ops, SparseCore 0:
  9.6 20.4 all-gather.9
  31.6 21.8 all-gather.7
  56.3 42.0 all-gather.19
  101.0 40.6 all-gather.11
  143.1 20.5 all-gather.13
  165.1 66.4 all-gather.15
  233.1 38.5 all-gather.17
  315.1 70.9 reduce-scatter.11
  389.7 69.5 reduce-scatter.9
  462.2 29.5 reduce-scatter.13
  494.6 30.6 reduce-scatter.17
  527.7 26.0 reduce-scatter.15
  556.5 51.3 reduce-scatter.21
  610.4 80.9 reduce-scatter.19
where the time goes:
time: 1090 us; the launch traced here: 1080 us
  waiting for transfers between devices  473 us (43%)
  blocking collectives  400 us (37%)
  matrix products  126 us (12%)
  local copies, waits for them, and re-layouts  40.6 us (4%)
  other arithmetic  27.4 us (3%)
  between operations  17 us (2%)
    psum x1, blocking collectives, local(): lax.psum((owned[0], owned[1], owned[2], owned[3], owned[4], owned[5], own...  386 us
    reduce_scatter x2, waiting for transfers between devices, local(): lax.psum_scatter(dkv_blocks.reshape(seq_len, 2 * kv_width), 'ctx', scatte...  108 us
    reduce_scatter x1, waiting for transfers between devices, local(): lax.psum_scatter(grad_names[5].astype(jnp.bfloat16), 'wt', scatter_dimens...  81.4 us
    all_gather x2, waiting for transfers between devices, local(): kv_whole = lax.all_gather(kv_send, 'ctx', axis=0, tiled=True)  70.2 us
    all_gather x1, waiting for transfers between devices, local(): lax.all_gather(w_gu, 'wt', axis=0, tiled=True)  63 us
    unnamed x15, waiting for transfers between devices  57.4 us
    dot_general x10, matrix products, outer_sum(): lax.dot_general(left, right, (((0,), (0,)), ((), ())), preferred_element_...  35.2 us
    all_gather x1, waiting for transfers between devices, local(): lax.all_gather(w_down, 'wt', axis=0, tiled=True)  29.9 us
  transfers between devices with their start and end apart: 14, of which 13 were waited for; matrix products, arithmetic and copies ran while one was open for 14% of the time, Pallas kernels for 0%

commit v1 on v0

--- a/solution.py
+++ b/solution.py
@@ -1,8 +1,12 @@
 import math
+
+import functools
 
 import jax
 import jax.numpy as jnp
 from jax import lax
+from jax.experimental import pallas as pl
+from jax.experimental.pallas import tpu as pltpu
 from jax.sharding import PartitionSpec as P
 
 QH = 15
@@ -84,7 +88,7 @@
     return (scores, visible)
 
 
-def local(hidden_in, d_out, block_order, gain_attn, gain_mlp, w_q, w_kv, w_o, w_gu, w_down):
+def local_general(hidden_in, d_out, block_order, gain_attn, gain_mlp, w_q, w_kv, w_o, w_gu, w_down):
     gathered = (
         lax.all_gather(gain_attn, "wt", axis=0, tiled=True),
         lax.all_gather(gain_mlp, "wt", axis=0, tiled=True),
@@ -331,6 +335,670 @@
     )
 
 
+MESH = pl.DeviceIdType.MESH
+ANY = pl.BlockSpec(memory_space=pl.ANY)
+VMEM = pl.BlockSpec(memory_space=pltpu.VMEM)
+BF = jnp.bfloat16
+F32 = jnp.float32
+
+
+class Place:
+    def __init__(self):
+        ctx = lax.axis_index("ctx")
+        wt = lax.axis_index("wt")
+        self.ctx, self.wt = ctx, wt
+        self.z, self.x = ctx // 2, ctx % 2
+        self.y, self.c = wt // 2, wt % 2
+
+    def dev(self, z=None, x=None, y=None, c=None):
+        z = self.z if z is None else z
+        x = self.x if x is None else x
+        y = self.y if y is None else y
+        c = self.c if c is None else c
+        return {"ctx": z * 2 + x, "wt": y * 2 + c}
+
+
+def barrier(devices):
+    sem = pltpu.get_barrier_semaphore()
+    for device in devices:
+        pl.semaphore_signal(sem, inc=1, device_id=device, device_id_type=MESH)
+    pl.semaphore_wait(sem, len(devices))
+
+
+class Copies:
+    def __init__(self, send, recv, local=None):
+        self.send, self.recv, self.local = send, recv, local
+        self.used = 0
+        self.used_local = 0
+
+    def remote(self, src, dst, device):
+        index = self.used
+        self.used += 1
+        return pltpu.make_async_remote_copy(
+            src_ref=src,
+            dst_ref=dst,
+            send_sem=self.send.at[index],
+            recv_sem=self.recv.at[index],
+            device_id=device,
+            device_id_type=MESH,
+        )
+
+    def near(self, src, dst):
+        index = self.used_local
+        self.used_local += 1
+        return pltpu.make_async_copy(src, dst, self.local.at[index])
+
+
+def rows_of(index, size):
+    return pl.ds(pl.multiple_of(index * size, size), size)
+
+
+class Gather:
+    def __init__(self, copies, place, axis, src, ref):
+        me = getattr(place, axis)
+        own = me * 2 + place.c
+        across = (1 - me) * 2 + place.c
+        self.place = place
+        partner = place.dev(c=1 - place.c)
+        self.far = copies.remote(src, ref.at[own], place.dev(**{axis: 1 - me}))
+        self.near = copies.remote(src, ref.at[own], partner)
+        self.relay = copies.remote(ref.at[across], ref.at[across], partner)
+        self.far.start()
+        self.near.start()
+
+    def pass_on(self):
+        self.far.wait_recv()
+        self.relay.start()
+
+    def wait(self):
+        self.near.wait_recv()
+        self.relay.wait_recv()
+        self.far.wait_send()
+        self.near.wait_send()
+        self.relay.wait_send()
+
+
+def start_kernel(hid, dout, wq, wkv, wo, wgu, gains, xs, dos, wq_o, wkv_o, wo_o, wgu_o, gains_o, send, recv, local, zsend, zrecv, zlocal):
+    at = Place()
+    z, x, y, c = at.z, at.x, at.y, at.c
+    partners = [at.dev(c=1 - c), at.dev(y=1 - y), at.dev(y=1 - y, c=1 - c)]
+    for step in (1, 2, 3):
+        for core in (0, 1):
+            partners.append(at.dev(z=(z + step) % 4, c=core))
+    barrier(partners)
+    copies = Copies(send, recv, local)
+    own = at.wt
+
+    def move(source, target, base):
+        for micro in range(2):
+            to_z = 2 * micro + c
+            core = z // 2
+            here = (to_z == z) & (core == c)
+            slot = z % 2
+
+            @pl.when(here)
+            def _():
+                pltpu.make_async_copy(source.at[micro, 0], target(c, slot), zlocal.at[base]).start()
+
+            @pl.when(jnp.logical_not(here))
+            def _():
+                pltpu.make_async_remote_copy(
+                    src_ref=source.at[micro, 0],
+                    dst_ref=target(core, slot),
+                    send_sem=zsend.at[base * 2 + micro],
+                    recv_sem=zrecv.at[base * 2 + slot],
+                    device_id=at.dev(z=to_z, c=core),
+                    device_id_type=MESH,
+                ).start()
+
+    def move_wait(source, target, base):
+        for micro in range(2):
+            here = (2 * micro + c == z) & (z // 2 == c)
+
+            @pl.when(jnp.logical_not(here))
+            def _():
+                pltpu.make_async_remote_copy(
+                    src_ref=source.at[micro, 0],
+                    dst_ref=target(c, 0),
+                    send_sem=zsend.at[base * 2 + micro],
+                    recv_sem=zrecv.at[base * 2],
+                    device_id=at.dev(c=1 - c),
+                    device_id_type=MESH,
+                ).wait_send()
+
+        for slot in range(2):
+            here = (2 * c + slot == z) & (z % 2 == c)
+
+            @pl.when(here)
+            def _():
+                pltpu.make_async_copy(source.at[0, 0], target(c, slot), zlocal.at[base]).wait()
+
+            @pl.when(jnp.logical_not(here))
+            def _():
+                pltpu.make_async_remote_copy(
+                    src_ref=source.at[0, 0],
+                    dst_ref=target(c, slot),
+                    send_sem=zsend.at[base * 2],
+                    recv_sem=zrecv.at[base * 2 + slot],
+                    device_id=at.dev(c=1 - c),
+                    device_id_type=MESH,
+                ).wait_recv()
+
+    move(hid, lambda core, slot: xs.at[slot], 0)
+    move(dout, lambda core, slot: dos.at[y * 2 + core, slot], 1)
+    gathers = []
+    locals_ = []
+    for src, dst in ((gains, gains_o), (wq, wq_o), (wkv, wkv_o), (wo, wo_o)):
+        gathers.append(Gather(copies, at, "y", src, dst))
+        mine = copies.near(src, dst.at[own])
+        mine.start()
+        locals_.append(mine)
+    columns = []
+    for part in range(2):
+        for y_to, c_to in ((1 - y, c), (1 - y, 1 - c), (y, 1 - c)):
+            to = y_to * 2 + c_to
+            copy = copies.remote(
+                wgu.at[:, rows_of(part * 4 + to, 640)],
+                wgu_o.at[own, :, pl.ds(part * 640, 640)],
+                at.dev(y=y_to, c=c_to),
+            )
+            copy.start()
+            columns.append(copy)
+        mine = copies.near(wgu.at[:, rows_of(part * 4 + own, 640)], wgu_o.at[own, :, pl.ds(part * 640, 640)])
+        mine.start()
+        locals_.append(mine)
+    move_wait(hid, lambda core, slot: xs.at[slot], 0)
+    for gather in gathers:
+        gather.pass_on()
+    move_wait(dout, lambda core, slot: dos.at[y * 2 + core, slot], 1)
+    gathers.append(Gather(copies, at, "y", dos.at[own], dos))
+    gathers[-1].pass_on()
+    for gather in gathers:
+        gather.wait()
+    for copy in columns:
+        copy.wait_recv()
+        copy.wait_send()
+    for copy in locals_:
+        copy.wait()
+
+
+def gather_kernel(axis, src, out, send, recv, local):
+    at = Place()
+    me = getattr(at, axis)
+    barrier([at.dev(c=1 - at.c), at.dev(**{axis: 1 - me})])
+    copies = Copies(send, recv, local)
+    gather = Gather(copies, at, axis, src, out)
+    mine = copies.near(src, out.at[me * 2 + at.c])
+    mine.start()
+    gather.pass_on()
+    gather.wait()
+    mine.wait()
+
+
+def gather_call(axis, src, collective):
+    return pl.pallas_call(
+        functools.partial(gather_kernel, axis),
+        out_shape=jax.ShapeDtypeStruct((4,) + src.shape, src.dtype),
+        in_specs=[VMEM],
+        out_specs=VMEM,
+        scratch_shapes=[
+            pltpu.SemaphoreType.DMA((3,)),
+            pltpu.SemaphoreType.DMA((3,)),
+            pltpu.SemaphoreType.DMA((1,)),
+        ],
+        compiler_params=pltpu.CompilerParams(collective_id=collective, has_side_effects=True),
+    )(src)
+
+
+class Scatter:
+    def __init__(self, copies, place, axis, part, one, two, three, total):
+        me = getattr(place, axis)
+        c = place.c
+        self.me, self.c, self.part = me, c, part
+        self.one, self.two, self.three, self.total = one, two, three, total
+        partner = place.dev(c=1 - c)
+        self.first = copies.remote(part.at[(1 - me) * 2 + 1 - c], one, partner)
+        self.second = copies.remote(part.at[me * 2 + 1 - c], two, partner)
+        self.across = copies.remote(total, three, place.dev(**{axis: 1 - me}))
+
+    def start(self):
+        self.first.start()
+        self.second.start()
+
+    def middle(self):
+        self.first.wait_recv()
+        mine = self.part[(1 - self.me) * 2 + self.c].astype(F32)
+        self.total[...] = (mine + self.one[...].astype(F32)).astype(self.total.dtype)
+        self.across.start()
+
+    def finish(self):
+        self.second.wait_recv()
+        self.across.wait_recv()
+        mine = self.part[self.me * 2 + self.c].astype(F32)
+        value = mine + self.two[...].astype(F32) + self.three[...].astype(F32)
+        self.first.wait_send()
+        self.second.wait_send()
+        self.across.wait_send()
+        return value
+
+
+def scatter_kernel(axis, count, *refs):
+    parts, outs = refs[:count], refs[count : 2 * count]
+    slots = refs[2 * count : 6 * count]
+    send, recv = refs[6 * count :]
+    at = Place()
+    me = getattr(at, axis)
+    barrier([at.dev(c=1 - at.c), at.dev(**{axis: 1 - me})])
+    copies = Copies(send, recv)
+    scatters = [Scatter(copies, at, axis, parts[i], *slots[4 * i : 4 * i + 4]) for i in range(count)]
+    for item in scatters:
+        item.start()
+    for item in scatters:
+        item.middle()
+    for item, out in zip(scatters, outs):
+        out[...] = item.finish()
+
+
+def scatter_call(axis, parts, collective):
+    shapes = [part.shape[1:] for part in parts]
+    slots = []
+    for shape in shapes:
+        slots += [pltpu.VMEM(shape, BF)] * 4
+    return pl.pallas_call(
+        functools.partial(scatter_kernel, axis, len(parts)),
+        out_shape=[jax.ShapeDtypeStruct(shape, F32) for shape in shapes],
+        in_specs=[VMEM] * len(parts),
+        out_specs=[VMEM] * len(parts),
+        scratch_shapes=slots
+        + [
+            pltpu.SemaphoreType.DMA((3 * len(parts),)),
+            pltpu.SemaphoreType.DMA((3 * len(parts),)),
+        ],
+        compiler_params=pltpu.CompilerParams(collective_id=collective, has_side_effects=True),
+    )(*parts)
+
+
+class Halving:
+    def __init__(self, copies, place, src, dim, slots, sums, piece):
+        self.copies, self.place, self.src, self.dim = copies, place, src, dim
+        self.slots, self.sums, self.piece = slots, sums, piece
+        z = place.z
+        self.bits = (place.x, z % 2, z // 2)
+        self.partners = (
+            place.dev(x=1 - place.x),
+            place.dev(z=z + 1 - 2 * (z % 2)),
+            place.dev(z=z + 2 - 4 * (z // 2)),
+        )
+        self.size = src.shape[dim]
+        self.pending = None
+
+    def view(self, ref, index, size):
+        if self.dim == 0:
+            return ref.at[rows_of(index, size)]
+        return ref.at[:, rows_of(index, size)]
+
+    def source(self, stage):
+        return self.src if stage == 0 else self.sums[stage - 1]
+
+    def send(self, stage):
+        size = self.size >> (stage + 1)
+        self.pending = self.copies.remote(
+            self.view(self.source(stage), 1 - self.bits[stage], size), self.slots[stage], self.partners[stage]
+        )
+        self.pending.start()
+
+    def add(self, stage):
+        size = self.size >> (stage + 1)
+        self.pending.wait_recv()
+        mine = self.view(self.source(stage), self.bits[stage], size)[...].astype(F32)
+        target = self.piece if stage == 2 else self.sums[stage]
+        target[...] = (mine + self.slots[stage][...].astype(F32)).astype(BF)
+        self.pending.wait_send()
+
+
+class Doubling:
+    def __init__(self, copies, place, out, dim):
+        self.copies, self.place, self.out, self.dim = copies, place, out, dim
+        z = place.z
+        self.index = place.x * 4 + (z % 2) * 2 + z // 2
+        self.partners = (
+            place.dev(x=1 - place.x),
+            place.dev(z=z + 1 - 2 * (z % 2)),
+            place.dev(z=z + 2 - 4 * (z // 2)),
+        )
+        self.size = out.shape[dim]
+
+    def view(self, index, size):
+        if self.dim == 0:
+            return self.out.at[rows_of(index, size)]
+        return self.out.at[:, rows_of(index, size)]
+
+    def send(self, stage):
+        size = self.size >> (stage + 1)
+        index = self.index // (1 << (2 - stage))
+        view = self.view(index, size)
+        self.pending = self.copies.remote(view, view, self.partners[stage])
+        self.pending.start()
+
+    def wait(self):
+        self.pending.wait_recv()
+        self.pending.wait_send()
+
+
+def end_kernel(
+    qkvo, gu, down, ho, gi,
+    down_o, gu_o, qkvo_o, ho_o, gi_o,
+    w1, w2, w3, w4, qkvo_own,
+    d1, d2, d3, ds1, ds2, g1, g2, g3, gs1, gs2, gp, q1, q2, q3, qs1, qs2,
+    send, recv, local, zsend, zrecv, zlocal,
+):
+    at = Place()
+    z, x, y, c = at.z, at.x, at.y, at.c
+    partners = [
+        at.dev(c=1 - c), at.dev(y=1 - y), at.dev(y=1 - y, c=1 - c), at.dev(x=1 - x),
+    ]
+    for step in (1, 2, 3):
+        for core in (0, 1):
+            partners.append(at.dev(z=(z + step) % 4, c=core))
+    barrier(partners)
+    copies = Copies(send, recv, local)
+
+    def back(source, target, base):
+        for slot in range(2):
+            to_z = 2 * c + slot
+            core = z % 2
+            here = (to_z == z) & (core == c)
+            micro = z // 2
+
+            @pl.when(here)
+            def _():
+                pltpu.make_async_copy(source.at[slot], target.at[micro, 0], zlocal.at[base]).start()
+
+            @pl.when(jnp.logical_not(here))
+            def _():
+                pltpu.make_async_remote_copy(
+                    src_ref=source.at[slot],
+                    dst_ref=target.at[micro, 0],
+                    send_sem=zsend.at[base * 2 + slot],
+                    recv_sem=zrecv.at[base * 2 + micro],
+                    device_id=at.dev(z=to_z, c=core),
+                    device_id_type=MESH,
+                ).start()
+
+    def back_wait(source, target, base):
+        for slot in range(2):
+            here = (2 * c + slot == z) & (z % 2 == c)
+
+            @pl.when(jnp.logical_not(here))
+            def _():
+                pltpu.make_async_remote_copy(
+                    src_ref=source.at[slot],
+                    dst_ref=target.at[0, 0],
+                    send_sem=zsend.at[base * 2 + slot],
+                    recv_sem=zrecv.at[base * 2],
+                    device_id=at.dev(c=1 - c),
+                    device_id_type=MESH,
+                ).wait_send()
+
+        for micro in range(2):
+            here = (2 * micro + c == z) & (z // 2 == c)
+
+            @pl.when(here)
+            def _():
+                pltpu.make_async_copy(source.at[0], target.at[micro, 0], zlocal.at[base]).wait()
+
+            @pl.when(jnp.logical_not(here))
+            def _():
+                pltpu.make_async_remote_copy(
+                    src_ref=source.at[0],
+                    dst_ref=target.at[micro, 0],
+                    send_sem=zsend.at[base * 2],
+                    recv_sem=zrecv.at[base * 2 + micro],
+                    device_id=at.dev(c=1 - c),
+                    device_id_type=MESH,
+                ).wait_recv()
+
+    scatter = Scatter(copies, at, "y", qkvo, w1, w2, w3, w4)
+    scatter.start()
+    index = x * 4 + (z % 2) * 2 + z // 2
+    halves = [
+        Halving(copies, at, down, 0, (d1, d2, d3), (ds1, ds2), down_o.at[rows_of(index, 80)]),
+        Halving(copies, at, gu, 1, (g1, g2, g3), (gs1, gs2), gp),
+    ]
+    for half in halves:
+        half.send(0)
+    back(ho, ho_o, 0)
+    back(gi, gi_o, 1)
+    scatter.middle()
+    for stage in range(3):
+        for half in halves:
+            half.add(stage)
+            if stage < 2:
+                half.send(stage + 1)
+    own = at.wt
+    down_back = Doubling(copies, at, down_o, 0)
+    down_back.send(2)
+    moved = []
+    for y_to, c_to in ((1 - y, c), (1 - y, 1 - c), (y, 1 - c)):
+        to = y_to * 2 + c_to
+        for part in range(2):
+            copy = copies.remote(
+                gp.at[to, :, pl.ds(part * 640, 640)],
+                gu_o.at[rows_of(index, 32), rows_of(part * 4 + own, 640)],
+                at.dev(y=y_to, c=c_to),
+            )
+            copy.start()
+            moved.append(copy)
+    for part in range(2):
+        gu_o[rows_of(index, 32), rows_of(part * 4 + own, 640)] = gp[own, :, part * 640 : part * 640 + 640]
+    qkvo_own[...] = scatter.finish().astype(BF)
+    third = Halving(copies, at, qkvo_own, 0, (q1, q2, q3), (qs1, qs2), qkvo_o.at[rows_of(index, 32)])
+    third.send(0)
+    down_back.wait()
+    down_back.send(1)
+    for copy in moved:
+        copy.wait_recv()
+        copy.wait_send()
+    gu_back = Doubling(copies, at, gu_o, 0)
+    gu_back.send(2)
+    third.add(0)
+    third.send(1)
+    down_back.wait()
+    down_back.send(0)
+    gu_back.wait()
+    gu_back.send(1)
+    third.add(1)
+    third.send(2)
+    third.add(2)
+    last = Doubling(copies, at, qkvo_o, 0)
+    last.send(2)
+    gu_back.wait()
+    gu_back.send(0)
+    last.wait()
+    last.send(1)
+    last.wait()
+    last.send(0)
+    down_back.wait()
+    gu_back.wait()
+    last.wait()
+    back_wait(ho, ho_o, 0)
+    back_wait(gi, gi_o, 1)
+
+
+def start_call(hid, dout, wq, wkv, wo, wgu, gains):
+    def out(shape):
+        return jax.ShapeDtypeStruct(shape, BF)
+
+    return pl.pallas_call(
+        start_kernel,
+        out_shape=[
+            out((2,) + hid.shape[2:]),
+            out((4, 2) + hid.shape[2:]),
+            out((4,) + wq.shape),
+            out((4,) + wkv.shape),
+            out((4,) + wo.shape),
+            out((4, wgu.shape[0], wgu.shape[1] // 4)),
+            out((4,) + gains.shape),
+        ],
+        in_specs=[ANY] * 7,
+        out_specs=[ANY] * 7,
+        scratch_shapes=[
+            pltpu.SemaphoreType.DMA((21,)),
+            pltpu.SemaphoreType.DMA((21,)),
+            pltpu.SemaphoreType.DMA((6,)),
+            pltpu.SemaphoreType.DMA((4,)),
+            pltpu.SemaphoreType.DMA((4,)),
+            pltpu.SemaphoreType.DMA((2,)),
+        ],
+        compiler_params=pltpu.CompilerParams(collective_id=0, has_side_effects=True),
+    )(hid, dout, wq, wkv, wo, wgu, gains)
+
+
+def end_call(qkvo, gu, down, ho, gi):
+    def out(shape):
+        return jax.ShapeDtypeStruct(shape, BF)
+
+    def buf(*shape):
+        return pltpu.VMEM(shape, BF)
+
+    micro = (2, 1) + ho.shape[1:]
+    return pl.pallas_call(
+        end_kernel,
+        out_shape=[out((640, 960)), out((256, 5120)), out((256, 2560)), out(micro), out(micro)],
+        in_specs=[VMEM] * 5,
+        out_specs=[VMEM] * 5,
+        scratch_shapes=[buf(256, 2560)] * 5
+        + [buf(320, 960), buf(160, 960), buf(80, 960), buf(320, 960), buf(160, 960)]
+        + [buf(4, 128, 1280), buf(4, 64, 1280), buf(4, 32, 1280), buf(4, 128, 1280), buf(4, 64, 1280), buf(4, 32, 1280)]
+        + [buf(128, 2560), buf(64, 2560), buf(32, 2560), buf(128, 2560), buf(64, 2560)]
+        + [
+            pltpu.SemaphoreType.DMA((40,)),
+            pltpu.SemaphoreType.DMA((40,)),
+            pltpu.SemaphoreType.DMA((2,)),
+            pltpu.SemaphoreType.DMA((4,)),
+            pltpu.SemaphoreType.DMA((4,)),
+            pltpu.SemaphoreType.DMA((2,)),
+        ],
+        compiler_params=pltpu.CompilerParams(
+            collective_id=6, has_side_effects=True, vmem_limit_bytes=60 * 1024 * 1024
+        ),
+    )(qkvo, gu, down, ho, gi)
+
+
+def local_fast(hidden_in, d_out, block_order, gain_attn, gain_mlp, w_q, w_kv, w_o, w_gu, w_down):
+    at = Place()
+    seg = hidden_in.shape[2]
+    width = hidden_in.shape[3]
+    half_block = seg // 2
+    rows = 2 * seg
+    kv_width = KVH * HD
+    group_size = QH // KVH
+    score_scale = 1.0 / math.sqrt(HD)
+    gains = jnp.zeros((16, 256), BF).at[0, :240].set(gain_attn).at[1, :240].set(gain_mlp)
+    xs, dos, wq, wkv, wo, wgu, gains_all = start_call(hidden_in, d_out, w_q, w_kv, w_o, w_gu, gains)
+    gain_one = gains_all[:, 0, :240].reshape(width).astype(F32)
+    gain_two = gains_all[:, 1, :240].reshape(width).astype(F32)
+    wq = wq.reshape(width, width)
+    wkv = wkv.reshape(width, 2 * kv_width)
+    wo = wo.reshape(width, width)
+    wgu = wgu.reshape(width, -1)
+    dos = dos.reshape(4 * rows, width)
+
+    order = lax.dynamic_index_in_dim(block_order, at.z // 2, 0, keepdims=False).reshape(4, 2, 2)
+    key_pos = (
+        order.transpose(1, 0, 2)[..., None] * half_block + jnp.arange(half_block, dtype=jnp.int32)
+    ).reshape(4 * rows)
+    row_pos = lax.dynamic_slice_in_dim(key_pos, (at.x * 2 + at.c) * rows, rows)
+    cosine, sine = rope_tables(row_pos)
+
+    tokens = xs.reshape(rows, width).astype(F32)
+    normed_one, pull_one = jax.vjp(norm_scale, tokens, gain_one)
+    act_one = normed_one.astype(BF)
+    query = jnp.dot(act_one, wq, preferred_element_type=F32).reshape(rows, QH, HD)
+    query = rotate(query, cosine, sine).astype(BF)
+    query = query.reshape(rows, KVH, group_size, HD).transpose(1, 2, 0, 3)
+    kv_lin = jnp.dot(act_one, wkv, preferred_element_type=F32)
+    key_rot = rotate(kv_lin[:, :kv_width].reshape(rows, KVH, HD), cosine, sine).reshape(rows, kv_width)
+    kv_mine = jnp.concatenate([key_rot, kv_lin[:, kv_width:]], axis=1).astype(BF)
+    kv_all = gather_call("x", kv_mine, 1).reshape(4 * rows, 2 * kv_width)
+    keys = kv_all[:, :kv_width].reshape(4 * rows, KVH, HD)
+    vals = kv_all[:, kv_width:].reshape(4 * rows, KVH, HD)
+    visible = key_pos[None, :] <= row_pos[:, None]
+
+    scores = jnp.einsum("grqd,kgd->grqk", query, keys, preferred_element_type=F32) * score_scale
+    scores = jnp.where(visible, scores, -1e30)
+    top = jnp.max(scores, axis=-1, keepdims=True)
+    probs = jnp.where(visible, jnp.exp(scores - top), 0.0)
+    probs = probs / jnp.sum(probs, axis=-1, keepdims=True)
+    attn = jnp.einsum("grqk,kgd->qgrd", probs.astype(BF), vals, preferred_element_type=F32)
+    attn = attn.reshape(rows, QH * HD).astype(BF)
+    mid = tokens + jnp.dot(attn, wo, preferred_element_type=F32)
+    normed_two, pull_two = jax.vjp(norm_scale, mid, gain_two)
+    act_two = gather_call("y", normed_two.astype(BF), 2).reshape(4 * rows, width)
+
+    gate_up = jnp.dot(act_two, wgu, preferred_element_type=F32)
+    ff = gate_up.shape[1] // 2
+    gate, up = gate_up[:, :ff], gate_up[:, ff:]
+    sig = jax.nn.sigmoid(gate)
+    hidden = (gate * sig * up).astype(BF)
+    out_part = jnp.dot(hidden, w_down, preferred_element_type=F32).astype(BF)
+    grad_down = outer_sum(hidden, dos)
+    d_hidden = back_product(dos, w_down)
+    d_gate = d_hidden * up * sig * (1.0 + gate * (1.0 - sig))
+    d_up = d_hidden * gate * sig
+    d_gu = jnp.concatenate([d_gate, d_up], axis=1).astype(BF)
+    grad_gu = outer_sum(act_two, d_gu)
+    d_part = back_product(d_gu, wgu).astype(BF)
+    out_sum, d_act_two = scatter_call(
+        "y", [out_part.reshape(4, rows, width), d_part.reshape(4, rows, width)], 3
+    )
+    result = (mid + out_sum).astype(BF)
+    d_mid_norm, grad_gain_two = pull_two(d_act_two)
+    d_own = lax.dynamic_slice_in_dim(dos, at.wt * rows, rows).astype(F32)
+    d_mid = d_own + d_mid_norm
+    d_mid_low = d_mid.astype(BF)
+    grad_o = outer_sum(attn, d_mid_low)
+    d_attn = back_product(d_mid_low, wo).astype(BF)
+    d_attn = d_attn.reshape(rows, KVH, group_size, HD).transpose(1, 2, 0, 3)
+    d_probs = jnp.einsum("grqd,kgd->grqk", d_attn, vals, preferred_element_type=F32)
+    delta = jnp.sum(probs * d_probs, axis=-1, keepdims=True)
+    d_scores = (probs * (d_probs - delta)).astype(BF)
+    d_query = jnp.einsum("grqk,kgd->qgrd", d_scores, keys, preferred_element_type=F32) * score_scale
+    d_keys = jnp.einsum("grqk,grqd->kgd", d_scores, query, preferred_element_type=F32) * score_scale
+    d_vals = jnp.einsum("grqk,grqd->kgd", probs.astype(BF), d_attn, preferred_element_type=F32)
+    d_kv = jnp.concatenate([d_keys.reshape(4 * rows, kv_width), d_vals.reshape(4 * rows, kv_width)], axis=1)
+    (d_kv,) = scatter_call("x", [d_kv.astype(BF).reshape(4, rows, 2 * kv_width)], 4)
+    d_q_low = unrotate(d_query.reshape(rows, QH, HD), cosine, sine).reshape(rows, QH * HD).astype(BF)
+    d_key = unrotate(d_kv[:, :kv_width].reshape(rows, KVH, HD), cosine, sine).reshape(rows, kv_width)
+    d_kv_low = jnp.concatenate([d_key, d_kv[:, kv_width:]], axis=1).astype(BF)
+    d_qkv = jnp.concatenate([d_q_low, d_kv_low], axis=1)
+    grad_qkv = outer_sum(act_one, d_qkv)
+    d_act_one = back_product(d_q_low, wq) + back_product(d_kv_low, wkv)
+    d_in_norm, grad_gain_one = pull_one(d_act_one)
+    grad_in = (d_mid + d_in_norm).astype(BF)
+
+    qkvo = jnp.concatenate([grad_qkv, grad_o], axis=1).reshape(4, 240, 2560)
+    tail = jnp.stack([grad_gain_one, grad_gain_two]).reshape(2, 4, 240).transpose(1, 0, 2)
+    tail = jnp.pad(tail, ((0, 0), (0, 14), (0, 2560 - 240)))
+    qkvo = jnp.concatenate([qkvo, tail], axis=1).astype(BF)
+    gu = jnp.pad(grad_gu.reshape(4, 240, -1), ((0, 0), (0, 16), (0, 0))).astype(BF)
+    down_o, gu_o, qkvo_o, hidden_out, grad_in = end_call(
+        qkvo, gu, grad_down.astype(BF), result.reshape(2, seg, width), grad_in.reshape(2, seg, width)
+    )
+    qkvo_o = qkvo_o.astype(F32)
+    return (
+        hidden_out,
+        grad_in,
+        qkvo_o[240, :240],
+        qkvo_o[241, :240],
+        qkvo_o[:240, :960],
+        qkvo_o[:240, 960:1600],
+        qkvo_o[:240, 1600:],
+        gu_o[:240].astype(F32),
+        down_o.astype(F32),
+    )
+
+
 def solution(mesh):
     placed = (
         P(None, "wt", "ctx", None),
@@ -344,6 +1012,7 @@
         P("wt", None),
         P("wt", None),
     )
+    local = local_fast if dict(mesh.shape) == {"ctx": 8, "wt": 4} else local_general
     return jax.shard_map(
         local,
         mesh=mesh,

time: 1090 us -> 517 us (0.47)
  waiting for transfers between devices: 473 us -> 0 us
  blocking collectives: 400 us -> 0 us
  Pallas kernels: 0 us -> 334 us
  matrix products: 126 us -> 82.8 us
  local copies, waits for them, and re-layouts: 40.6 us -> 61.8 us
  between operations: 17 us -> 1.47 us
    psum x1 -> x0, blocking collectives: 386 us -> none  [local(): lax.psum((owned[0], owned[1], owned[2], owned[3], owned[4], owned[5], own...]
    pallas_call x0 -> x6, Pallas kernels: none -> 334 us  [the longest x1 177 us: end_call(): pl.pallas_call(end_kernel, out_shape=[out((640, 960)), out((256, 5120)),...]
    reduce_scatter x6 -> x0, waiting for transfers between devices: 219 us -> none  [the longest x2 108 us: local(): lax.psum_scatter(dkv_blocks.reshape(seq_len, 2 * kv_width), 'ctx', scatte...]
    all_gather x7 -> x0, waiting for transfers between devices: 196 us -> none  [the longest x2 70.2 us: local(): kv_whole = lax.all_gather(kv_send, 'ctx', axis=0, tiled=True)]
    unnamed x15 -> x0, waiting for transfers between devices: 57.4 us -> none
    dot_general x10 -> x4, matrix products: 35.2 us -> 11 us  [outer_sum(): lax.dot_general(left, right, (((0,), (0,)), ((), ())), preferred_element_...]
    dot_general x22 -> x10, matrix products: 64 us -> 46.5 us  [the longest x1 12.8 us: local_fast(): jnp.einsum('grqd,kgd->grqk', d_attn, vals, preferred_element_type=F32)]
    unnamed x2 -> x0, blocking collectives: 14.1 us -> none
  transfers between devices with their start and end apart: 14 -> 0, of which waited for: 13 -> 0; matrix products, arithmetic and copies ran while one was open for 14% -> 0% of each run, Pallas kernels for 0% -> 0%
where the time goes in v1:
time: 517 us; the launch traced here: 512 us
  Pallas kernels  334 us (65%)
  matrix products  82.8 us (16%)
  local copies, waits for them, and re-layouts  61.8 us (12%)
  other arithmetic  32.3 us (6%)
    pallas_call x1, Pallas kernels, end_call(): pl.pallas_call(end_kernel, out_shape=[out((640, 960)), out((256, 5120)),...  177 us
    pallas_call x1, Pallas kernels, start_call(): pl.pallas_call(start_kernel, out_shape=[out((2,) + hid.shape[2:]), out((4...  80.5 us
    pallas_call x2, Pallas kernels, scatter_call(): pl.pallas_call(functools.partial(scatter_kernel, axis, len(parts)), out_s...  45.1 us
    pallas_call x2, Pallas kernels, gather_call(): pl.pallas_call(functools.partial(gather_kernel, axis), out_shape=jax.Shap...  31.4 us
    unnamed x63, local copies, waits for them, and re-layouts  15.1 us
    sub x1, matrix products, local_fast(): probs = jnp.where(visible, jnp.exp(scores - top), 0.0)  13.1 us
    dot_general x1, matrix products, local_fast(): jnp.einsum('grqd,kgd->grqk', d_attn, vals, preferred_element_type=F32)  12.8 us
    dot_general x5, matrix products, back_product(): lax.dot_general(left, weight, (((1,), (1,)), ((), ())), preferred_element...  12.2 us

profile of v1, /device:TPU:0, one launch (start us, length us, event | category | flops | bytes accessed | tf_op | source)
XLA Modules:
  0.0 512.1 jit_solution(4549613952222549507)
XLA Ops:
  8.5 80.5 %shard_map.169 = (bf16[2,128,960]{2,1,0:T(8,128)(2,1)}, bf16[4,2,128,960]{3,2,1,0:T(8,128)(2,1)}, bf16[4,240,960]{2,1,0:T(8,128)(2,1)}, bf16[4,240,640]{2,1,0:T(...) custom-call(bf16[2,1,128,960]{3,2,1,0:T(8,128)(2,1)} %copy.72.hid, ...), custom_call_target="tpu_custom_call" | custom-call | tf_op jit(solution)/shard_map/pallas_call | solution.py:832
  96.6 13.2 %shard_map.170 = bf16[4,256,640]{2,1,0:T(8,128)(2,1)} custom-call(bf16[256,640]{1,0:T(8,128)(2,1)} %pad_maximum_fusion.5.src), custom_call_target="tpu_custom_call" | custom-call | tf_op jit(solution)/shard_map/pallas_call | solution.py:539
  113.8 3.1 copy.78
  118.9 13.1 %fusion.68 = (f32[5,3,256]{2,1,0:T(4,128)S(1)}, f32[5,3,256,1024]{3,2,1,0:T(8,128)}) fusion(pred[256,1024]{1,0:T(8,128)(4,1)} %broadcast_compare_fusion, bf16[1024,5,64,1]{0,2,3,1:T(8,128)(2,1)} %bitcast.166, bf16[256,5,3,32]{0,3,2,1:T(8,128)(2,1)S(1)} %bitcast.181, bf16[256,5,3,32]{0,3,2,1:T(8,128)(2,1)S(1)} %bitcast.179), kind=kOutput, calls=%fused_computation.124 | convolution fusion | flops 523961344 | bytes 17153024 | tf_op jit(solution)/shard_map/sub | solution.py:931
  132.0 8.2 %fusion.22 = bf16[5,64,3,256]{3,1,2,0:T(8,128)(2,1)S(1)} fusion(bf16[1024,5,64,1]{0,2,3,1:T(8,128)(2,1)S(1)} %bitcast.184, f32[5,3,256,1024]{3,2,1,0:T(8,128)} %get-tuple-element.120, f32[5,3,256]{2,1,0:T(4,128)S(1)} %get-tuple-element.119), kind=kOutput, calls=%fused_computation.44 | convolution fusion | flops 511426560 | bytes 16890880 | tf_op jit(solution)/shard_map/grqk,kgd->qgrd/dot_general | solution.py:933
  142.0 18.2 %shard_map.171 = bf16[4,256,960]{2,1,0:T(8,128)(2,1)} custom-call(bf16[256,960]{1,0:T(8,128)(2,1)} %multiply_convert_fusion.4.src), custom_call_target="tpu_custom_call" | custom-call | tf_op jit(solution)/shard_map/pallas_call | solution.py:539
  160.2 4.4 copy.95
  164.7 5.3 %fusion.71 = f32[1024,1280]{1,0:T(8,128)S(1)} fusion(bf16[1024,960]{1,0:T(8,128)(2,1)} %bitcast.153, bf16[960,1280]{1,0:T(8,128)(2,1)} %bitcast.194), kind=kOutput, calls=%fused_computation.127 | convolution fusion | flops 2516582400 | bytes 9666560 | tf_op jit(solution)/shard_map/dot_general | solution.py:939
  170.1 3.7 multiply_convert_fusion.2
  173.7 3.9 convolution_convert_fusion.2
  177.6 3.9 convolution_convert_fusion
  181.5 3.9 copy.85
  185.4 3.5 pad.19.gu
  188.9 2.8 convolution_convert_fusion.5
  191.8 2.5 copy.96.down
  194.2 4.3 convolution_convert_fusion.4
  198.6 4.0 copy.82
  202.6 31.4 %shard_map.172 = (f32[256,960]{1,0:T(8,128)}, f32[256,960]{1,0:T(8,128)}) custom-call(bf16[4,256,960]{2,1,0:T(8,128)(2,1)} %bitcast.155, bf16[4,256,960]{2,1,0:T(8,128)(2,1)} %bitcast.154), custom_call_target="tpu_custom_call" | custom-call | tf_op jit(solution)/shard_map/pallas_call | solution.py:607
  235.9 2.4 add_convert_fusion
  239.7 6.5 %fusion.25 = bf16[1024,5,64]{0,2,1:T(8,128)(2,1)S(1)} fusion(bf16[5,3,256,64]{2,3,1,0:T(8,128)(2,1)S(1)} %bitcast.186, f32[5,3,256,1024]{3,2,1,0:T(8,128)} %get-tuple-element.120, f32[5,3,256]{2,1,0:T(4,128)S(1)} %get-tuple-element.119), kind=kOutput, calls=%fused_computation.45 | convolution fusion | flops 511508480 | bytes 16890880 | tf_op jit(solution)/shard_map/grqk,grqd->kgd/dot_general | solution.py:968
  247.5 3.1 convolution_convert_fusion.3
  250.7 12.8 %multiply_reduce_fusion = (f32[5,3,256]{2,1,0:T(4,128)S(1)}, f32[5,3,256,1024]{3,2,1,0:T(8,128)}) fusion(f32[5,3,256,1024]{3,2,1,0:T(8,128)} %get-tuple-element.120, f32[5,3,256]{2,1,0:T(4,128)S(1)} %get-tuple-element.119, bf16[5,3,256,64]{2,3,1,0:T(8,128)(2,1)} %bitcast.187, bf16[1024,5,64,1]{0,2,3,1:T(8,128)(2,1)} %bitcast.183), kind=kOutput, calls=%fused_computation.2 | convolution fusion | flops 515109120 | bytes 32634880 | tf_op jit(solution)/shard_map/grqd,kgd->grqk/dot_general | solution.py:963
  265.3 7.1 %multiply_convert_fusion = bf16[5,3,256,1024]{3,2,1,0:T(8,128)(2,1)S(1)} fusion(f32[5,3,256,1024]{3,2,1,0:T(8,128)} %get-tuple-element.124, f32[5,3,256]{2,1,0:T(4,128)S(1)} %get-tuple-element.123, f32[5,3,256,1024]{3,2,1,0:T(8,128)S(1)} %bitcast.149, f32[5,3,256]{2,1,0:T(4,128)S(1)} %get-tuple-element.119), kind=kLoop, calls=%fused_computation.1 | loop fusion | flops 15728640 | bytes 39352320 | tf_op jit(solution)/shard_map/convert_element_type | solution.py:965
  272.4 2.3 fusion.28
  274.8 2.5 convolution_multiply_fusion
  279.2 2.5 concatenate.66
  284.0 2.7 pad_maximum_fusion.4.refs_0_
  286.7 13.7 %shard_map.173 = f32[256,640]{1,0:T(8,128)} custom-call(bf16[4,256,640]{2,1,0:T(8,128)(2,1)} %pad_maximum_fusion.4.refs_0_), custom_call_target="tpu_custom_call" | custom-call | tf_op jit(solution)/shard_map/pallas_call | solution.py:607
  315.9 2.8 fusion.6.qkvo
  318.7 176.8 %shard_map.174 = (bf16[640,960]{1,0:T(8,128)(2,1)}, bf16[256,5120]{1,0:T(8,128)(2,1)}, bf16[256,2560]{1,0:T(8,128)(2,1)}, bf16[2,1,128,960]{3,2,1,0:T(8,128)(2,1)}, bf16[2,1,128,960]{3,2,1,0:T(8,128)(2,1)}) custom-call(bf16[4,256,2560]{2,1,0:T(8,128)(2,1)} %fusion.6.qkvo, bf16[4,256,1280]{2,1,0:T(8,128)(2,1)} %pad.19.gu, bf16[640,960]{1,0:T(8,128)(2,1)} %copy.96.down, ...), custom_call_target="tpu_custom_call" | custom-call | tf_op jit(solution)/shard_map/pallas_call | solution.py:865
  504.5 2.9 copy.99
  507.4 4.5 slice_convert_fusion
  (126 shorter events, 58.2 us)
Async XLA Ops:
  0.6 169.4 %copy-start = (bf16[640,960]{0,1:T(8,128)(2,1)S(1)}, bf16[640,960]{0,1:T(8,128)(2,1)}, u32[]{:S(2)}) copy-start(bf16[640,960]{0,1:T(8,128)(2,1)} %param.23) | copy-start | bytes 3686404
  3.4 5.2 %copy-start.22 = (bf16[16,256]{1,0:T(8,128)(2,1)}, bf16[16,256]{1,0:T(8,128)(2,1)S(1)}, u32[]{:S(2)}) copy-start(bf16[16,256]{1,0:T(8,128)(2,1)S(1)} %scatter.9.gains) | copy-start | bytes 24580
  92.5 0.8 copy-start.9
  118.9 13.1 %copy-start.15 = (bf16[256,15,32]{0,2,1:T(8,128)(2,1)}, bf16[256,15,32]{0,2,1:T(8,128)(2,1)S(1)}, u32[]{:S(2)}) copy-start(bf16[256,15,32]{0,2,1:T(8,128)(2,1)S(1)} %get-tuple-element.110) | copy-start | bytes 737284
  118.9 13.1 %copy-start.18 = (bf16[1024,320]{0,1:T(8,128)(2,1)S(1)}, bf16[1024,320]{0,1:T(8,128)(2,1)}, u32[]{:S(2)}) copy-start(bf16[1024,320]{0,1:T(8,128)(2,1)} %copy.80) | copy-start | bytes 1966084
  132.0 8.2 %copy-start.2 = (bf16[2,128,960]{2,1,0:T(8,128)(2,1)S(1)}, bf16[2,128,960]{2,1,0:T(8,128)(2,1)}, u32[]{:S(2)}) copy-start(bf16[2,128,960]{2,1,0:T(8,128)(2,1)} %get-tuple-element.47) | copy-start | bytes 1474564
  132.0 8.2 %copy-start.5 = (bf16[4,240,960]{2,1,0:T(8,128)(2,1)S(1)}, bf16[4,240,960]{2,1,0:T(8,128)(2,1)}, u32[]{:S(2)}) copy-start(bf16[4,240,960]{2,1,0:T(8,128)(2,1)} %get-tuple-element.52) | copy-start | bytes 5529604
  140.2 0.9 copy-start.13
  164.7 5.4 %copy-start.20 = (bf16[4,2,128,960]{3,2,1,0:T(8,128)(2,1)S(1)}, bf16[4,2,128,960]{3,2,1,0:T(8,128)(2,1)}, u32[]{:S(2)}) copy-start(bf16[4,2,128,960]{3,2,1,0:T(8,128)(2,1)} %get-tuple-element.51) | copy-start | bytes 5898244
  170.0 3.7 copy-start.23
  173.7 3.9 copy-start.12
  185.4 3.5 copy-start.21
  185.4 3.5 copy-start.24
  234.0 1.7 copy-start.11
  234.0 1.8 copy-start.14
  235.9 2.4 copy-start.6
  239.0 0.8 copy-start.19
  247.5 15.9 %slice-start = ((s8[15728640]{0:T(1024)(128)(4,1)}), s8[4194304]{0:T(1024)(128)(4,1)S(1)}, s32[]{:S(2)}) async-start(s8[15728640]{0:T(1024)(128)(4,1)} %bitcast.148), calls=%async_computation | async-start | bytes 8388608
  250.7 12.8 %slice-start.1 = ((s8[15728640]{0:T(1024)(128)(4,1)}), s8[4194304]{0:T(1024)(128)(4,1)S(1)}, s32[]{:S(2)}) async-start(s8[15728640]{0:T(1024)(128)(4,1)} %bitcast.148), calls=%async_computation.1 | async-start | bytes 8388608
  250.7 13.7 %slice-start.2 = ((s8[15728640]{0:T(1024)(128)(4,1)}), s8[4194304]{0:T(1024)(128)(4,1)S(1)}, s32[]{:S(2)}) async-start(s8[15728640]{0:T(1024)(128)(4,1)} %bitcast.148), calls=%async_computation.2 | async-start | bytes 8388608
  250.7 14.7 %slice-start.3 = ((s8[15728640]{0:T(1024)(128)(4,1)}), s8[3145728]{0:T(1024)(128)(4,1)S(1)}, s32[]{:S(2)}) async-start(s8[15728640]{0:T(1024)(128)(4,1)} %bitcast.148), calls=%async_computation.3 | async-start | bytes 6291456
  265.3 7.1 %copy-start.16 = (bf16[256,15,32]{0,2,1:T(8,128)(2,1)S(1)}, bf16[256,15,32]{0,2,1:T(8,128)(2,1)}, u32[]{:S(2)}) copy-start(bf16[256,15,32]{0,2,1:T(8,128)(2,1)} %copy-done.15) | copy-start | bytes 737284
  272.4 2.4 copy-start.10
  274.8 2.7 copy-start.4
  286.7 22.7 %copy-start.8 = (bf16[4,240,640]{2,1,0:T(8,128)(2,1)S(1)}, bf16[4,240,640]{2,1,0:T(8,128)(2,1)}, u32[]{:S(2)}) copy-start(bf16[4,240,640]{2,1,0:T(8,128)(2,1)} %get-tuple-element.49) | copy-start | bytes 3686404
  311.6 1.4 copy-start.17
  313.0 1.5 copy-start.3
  495.5 7.5 %copy-start.7 = (bf16[256,2560]{1,0:T(8,128)(2,1)S(1)}, bf16[256,2560]{1,0:T(8,128)(2,1)}, u32[]{:S(2)}) copy-start(bf16[256,2560]{1,0:T(8,128)(2,1)} %get-tuple-element.58) | copy-start | bytes 3932164
  504.5 7.4 %copy-start.1 = (bf16[640,960]{0,1:T(8,128)(2,1)S(1)}, bf16[640,960]{0,1:T(8,128)(2,1)}, u32[]{:S(2)}) copy-start(bf16[640,960]{0,1:T(8,128)(2,1)} %param.23) | copy-start | bytes 3686404
